TPU v7x, 256 devices: a whole 4x4x8 slice. The times are simulated.
256 devices in a mesh: row: 8 (over z_hi, x), col: 32 (over z_lo, y, core).
Axes of the slice: x: 4, y: 4, z: 8 (z_hi: 2, z_lo: 4; z = z_hi * 4 + z_lo), core: 2. Of those that a mesh axis runs over, the one named last changes fastest.
Arguments:
- object_field: float32 [2, 2048, 8192], P(None, 'row', 'col'), may hold values from -6 to 6
- probe: float32 [2, 4, 128, 128], replicated, may hold values from -6 to 6
- patterns: bfloat16 [8, 32, 8, 128, 128], P('row', 'col'), may hold values from 0.5 to 2
- row_scales: float32 [8, 32, 8, 128], P('row', 'col'), may hold values from 0.3 to 3
- positions: int32 [8, 32, 8, 2], P('row', 'col'), may hold values from 0 to 255
- counts: int32 [8, 32], P('row', 'col'), may hold values from 4 to 8, as said below
Outputs:
- object_out: float32 [2, 2048, 8192], P(None, 'row', 'col')
- probe_out: float32 [2, 4, 128, 128], replicated
Inputs may be any that keep to these rules, and one draw needn't show every extreme that they name: positions p >= counts[a,b] of tile (a,b) are ignored; some tile has all 8 positions live.
All inputs are finite; a program needn't handle non-finite values.
Results may differ from a plain program's by a relative error of at most 0.0003.
Values sent between devices are 32-bit elements; how exact they have to be, the bound alone decides.
No kernel may reach another device: no remote copies, remote signals or barrier semaphores. Data moves between devices by JAX's collectives and lax.ppermute only.
A program may use at most 128 MiB of HBM per device.

v0:
```python
import math
import jax
import jax.numpy as jnp
from jax import lax
from jax.sharding import PartitionSpec as P

PASSES = 2


def padded_2(block, sides, width):
    for axis, dim in sides:
        count = lax.axis_size(axis)
        forward = [(i, i + 1) for i in range(count - 1)]
        backward = [(target, source) for source, target in forward]
        low = lax.ppermute(
            lax.slice_in_dim(block, block.shape[dim] - width, None, axis=dim), axis, forward
        )
        high = lax.ppermute(lax.slice_in_dim(block, 0, width, axis=dim), axis, backward)
        block = jnp.concatenate([low, block, high], axis=dim)
    return block


def dft_tables(length):
    indices = lax.iota(jnp.int32, length)
    product = indices[:, None] * indices[None, :] % length
    angle = product.astype(jnp.float32) * (2.0 * math.pi / length)
    scaling = 1.0 / math.sqrt(length)
    cosine = jnp.cos(angle) * scaling
    sine_part = jnp.sin(angle) * scaling
    forward = jnp.concatenate(
        [jnp.concatenate([cosine, -sine_part], 1), jnp.concatenate([sine_part, cosine], 1)], 0
    )
    inverse = jnp.concatenate(
        [jnp.concatenate([cosine, sine_part], 1), jnp.concatenate([-sine_part, cosine], 1)], 0
    )
    return (forward, inverse)


def apply_table(waves, table):
    flattened = waves.reshape(-1, table.shape[0])
    result = jnp.dot(
        flattened, table, precision=lax.Precision.HIGHEST, preferred_element_type=jnp.float32
    )
    return result.reshape(waves.shape)


def transpose_pairs(waves):
    batch_size, length, pair_width = waves.shape
    return (
        waves.reshape(batch_size, length, 2, length)
        .transpose(0, 3, 2, 1)
        .reshape(batch_size, length, pair_width)
    )


def transform(waves, table):
    return transpose_pairs(apply_table(transpose_pairs(apply_table(waves, table)), table))


def fold_rim(padded, axis_number, inner, rim_width):
    middle = lax.slice_in_dim(padded, 2 * rim_width, 2 * rim_width + inner, axis=axis_number)
    lower = lax.slice_in_dim(padded, 0, rim_width, axis=axis_number)
    upper = lax.slice_in_dim(padded, inner + 3 * rim_width, inner + 4 * rim_width, axis=axis_number)
    head_part = lax.slice_in_dim(middle, 0, rim_width, axis=axis_number) + lower
    core_part = lax.slice_in_dim(middle, rim_width, inner - rim_width, axis=axis_number)
    tail_part = lax.slice_in_dim(middle, inner - rim_width, inner, axis=axis_number) + upper
    return jnp.concatenate([head_part, core_part, tail_part], axis=axis_number)


def on_device(object_field, probe, patterns, row_scales, positions, counts):
    modes = probe.shape[1]
    pattern_size = probe.shape[2]
    rim_width = pattern_size // 2
    tile_rows = object_field.shape[1]
    tile_cols = object_field.shape[2]
    position_count = positions.shape[2]
    forward, inverse = dft_tables(pattern_size)
    amplitudes = patterns[0, 0].astype(jnp.float32) * row_scales[0, 0][..., None]
    starts = positions[0, 0]
    live_flag = (lax.iota(jnp.int32, position_count) < counts[0, 0]).astype(jnp.float32)
    object_now = object_field
    probe_now = probe
    for pass_number in range(PASSES):
        extended = padded_2(object_now, (("row", 1), ("col", 2)), rim_width)
        patches = jax.vmap(
            lambda start_pair: lax.dynamic_slice(
                extended, (0, start_pair[0], start_pair[1]), (2, pattern_size, pattern_size)
            )
        )(starts)
        patch_re = patches[:, 0][:, None]
        patch_im = patches[:, 1][:, None]
        probe_re = probe_now[0][None]
        probe_im = probe_now[1][None]
        wave_re = probe_re * patch_re - probe_im * patch_im
        wave_im = probe_re * patch_im + probe_im * patch_re
        stacked = jnp.concatenate([wave_re, wave_im], axis=-1).reshape(
            -1, pattern_size, 2 * pattern_size
        )
        far_field = transform(stacked, forward).reshape(
            position_count, modes, pattern_size, 2 * pattern_size
        )
        far_re = far_field[..., :pattern_size]
        far_im = far_field[..., pattern_size:]
        intensity = jnp.sum(far_re * far_re + far_im * far_im, axis=1, keepdims=True)
        factor = amplitudes[:, None] / jnp.maximum(jnp.sqrt(intensity), 0.5)
        scaled = far_field * jnp.concatenate([factor, factor], axis=-1)
        back_wave = transform(scaled.reshape(-1, pattern_size, 2 * pattern_size), inverse)
        back_wave = back_wave.reshape(position_count, modes, pattern_size, 2 * pattern_size)
        live_mask = live_flag[:, None, None, None]
        diff_re = (back_wave[..., :pattern_size] - wave_re) * live_mask
        diff_im = (back_wave[..., pattern_size:] - wave_im) * live_mask
        contrib_re = jnp.sum(probe_re * diff_re + probe_im * diff_im, axis=1)
        contrib_im = jnp.sum(probe_re * diff_im - probe_im * diff_re, axis=1)
        updates = jnp.zeros((2, tile_rows + 2 * rim_width, tile_cols + 2 * rim_width), jnp.float32)
        for position in range(position_count):
            corner = (0, starts[position, 0], starts[position, 1])
            current = lax.dynamic_slice(updates, corner, (2, pattern_size, pattern_size))
            contribution = jnp.stack([contrib_re[position], contrib_im[position]])
            updates = lax.dynamic_update_slice(updates, current + contribution, corner)
        gradient_re = jnp.sum(patch_re * diff_re + patch_im * diff_im, axis=0)
        gradient_im = jnp.sum(patch_re * diff_im - patch_im * diff_re, axis=0)
        gradient = jnp.stack([gradient_re, gradient_im])
        weight = jnp.sum(
            live_flag[:, None, None] * (patches[:, 0] ** 2 + patches[:, 1] ** 2), axis=0
        )
        summed = padded_2(updates, (("row", 1), ("col", 2)), rim_width)
        tile_sum = fold_rim(fold_rim(summed, 1, tile_rows, rim_width), 2, tile_cols, rim_width)
        probe_peak = jnp.max(jnp.sum(probe_now[0] ** 2 + probe_now[1] ** 2, axis=0))
        object_now = object_now + tile_sum / probe_peak
        gradient_sum, weight_sum = lax.psum((gradient, weight), ("row", "col"))
        probe_now = probe_now + gradient_sum / weight_sum[None, None]
    return (object_now, probe_now)


def solution(mesh):
    placed = (
        P(None, "row", "col"),
        P(),
        P("row", "col", None, None, None),
        P("row", "col", None, None),
        P("row", "col", None, None),
        P("row", "col"),
    )
    return jax.shard_map(
        on_device,
        mesh=mesh,
        in_specs=placed,
        out_specs=(P(None, "row", "col"), P()),
        check_vma=False,
    )
```

profile of v0, /device:TPU:1, one launch (start us, length us, event | category | flops | bytes accessed | tf_op | source)
XLA Modules:
  0.0 857.3 jit_solution(2227831163460324998)
XLA Ops:
  8.2 3.9 collective-permute-start
  50.3 4.0 collective-permute-start.2
  59.1 4.4 collective-permute-done.3
  65.0 24.4 %while.2 = (s32[]{:T(128)}, f32[2,384,384]{2,1,0:T(8,128)}, s32[8,3]{0,1:T(4,128)S(1)}, f32[8,2,128,128]{3,2,0,1:T(8,128)S(1)}, s32[]{:T(128)}) while((s32[]{:T(128)}, f32[2,384,384]{2,1,0:T(8,128)}, s32[8,3]{0,1:T(4,128)S(1)}, f32[8,2,128,128]{3,2,0,1:T(8,128)S(1)}, s32[]{:T(128)}) %tuple.107), condition=%wide.while_cond, body=%wide.while_body.sunk | while | flops 2 | bytes 262261 | solution.py:86
  94.5 7.1 fusion.47
  104.6 7.1 fusion.48
  111.7 7.3 fusion.49
  126.1 4.9 add_reduce_fusion.2
  157.6 4.7 collective-permute-done.5
  168.8 3.8 collective-permute-done.6
  172.6 4.4 collective-permute-done.7
  182.4 9.1 %collective-permute-start.8 = (f32[2,64,256]{2,1,0:T(8,128)S(1)}, f32[2,64,256]{2,1,0:T(8,128)S(1)}, u32[]{:S(2)}, u32[]{:S(2)}) collective-permute-start(f32[2,64,256]{2,1,0:T(8,128)S(1)} %get-tuple-element.96), channel_id=1, source_target_pairs={{0,32},{32,64},{64,96},{96,128},{128,160},{160,192},{192,224},{1,3... | collective-permute-start | bytes 393224 | tf_op jit(solution)/shard_map/ppermute | solution.py:15
  193.5 11.1 %collective-permute-done.9 = f32[2,64,256]{2,1,0:T(8,128)S(1)} collective-permute-done((f32[2,64,256]{2,1,0:T(8,128)S(1)}, f32[2,64,256]{2,1,0:T(8,128)S(1)}, u32[]{:S(2)}, u32[]{:S(2)}) %collective-permute-start.9) | collective-permute-done | bytes 131104 | tf_op jit(solution)/shard_map/ppermute | solution.py:18
  214.3 4.4 collective-permute-done.11
  221.3 28.9 %while.3 = (s32[]{:T(128)}, f32[2,384,384]{2,1,0:T(8,128)}, s32[8,3]{0,1:T(4,128)S(1)}, f32[8,2,128,128]{3,2,1,0:T(8,128)}, s32[]{:T(128)}) while((s32[]{:T(128)}, f32[2,384,384]{2,1,0:T(8,128)}, s32[8,3]{0,1:T(4,128)S(1)}, f32[8,2,128,128]{3,2,1,0:T(8,128)}, s32[]{:T(128)}) %tuple.119), condition=%wide.while_cond.1, body=%wide.while_body.1.sunk | while | flops 2 | bytes 263785 | solution.py:86
  255.2 265.5 %all-reduce.7.cloned.1.call-done = (f32[2,4,128,128]{3,2,1,0:T(8,128)}, f32[128,128]{1,0:T(8,128)}) async-done(((f32[2,4,128,128]{3,2,1,0:T(8,128)}, f32[128,128]{1,0:T(8,128)}), (f32[2,4,128,128]{3,2,1,0:T(8,128)}, f32[128,128]{1,0:T(8,128)})) %all-reduce.7.cloned.1.call-update) | async-done | bytes 589840 | tf_op jit(solution)/shard_map/psum | solution.py:130
  522.6 3.7 fusion.3
  526.3 7.1 fusion.50
  536.0 7.1 fusion.51
  543.1 7.4 fusion.52
  557.6 4.8 add_reduce_fusion
  588.9 5.1 collective-permute-done.13
  595.1 5.1 collective-permute-start.14
  602.2 243.2 %all-reduce.5.cloned.1.call-done = (f32[2,4,128,128]{3,2,1,0:T(8,128)}, f32[128,128]{1,0:T(8,128)}) async-done(((f32[2,4,128,128]{3,2,1,0:T(8,128)}, f32[128,128]{1,0:T(8,128)}), (f32[2,4,128,128]{3,2,1,0:T(8,128)}, f32[128,128]{1,0:T(8,128)})) %all-reduce.5.cloned.1.call-update) | async-done | bytes 589840 | tf_op jit(solution)/shard_map/psum | solution.py:130
  (221 shorter events, 184.9 us)
Async XLA Ops:
  7.2 513.5 %all-reduce.7.cloned.1.call-start = ((), (), s32[]{:S(2)}) async-start(), calls=%async_computation.1 | async-start | bytes 1179648 | tf_op jit(solution)/shard_map/psum | solution.py:130
  8.2 40.8 %collective-permute-start = (f32[2,64,256]{2,1,0:T(8,128)S(1)}, f32[2,64,256]{2,1,0:T(8,128)S(1)}, u32[]{:S(2)}, u32[]{:S(2)}) collective-permute-start(f32[2,64,256]{2,1,0:T(8,128)S(1)} %get-tuple-element.117), channel_id=1, source_target_pairs={{0,32},{32,64},{64,96},{96,128},{128,160},{160,192},{192,224},{1,3... | collective-permute-start | bytes 393224 | tf_op jit(solution)/shard_map/ppermute | solution.py:15
  12.2 38.0 %collective-permute-start.1 = (f32[2,64,256]{2,1,0:T(8,128)S(1)}, f32[2,64,256]{2,1,0:T(8,128)S(1)}, u32[]{:S(2)}, u32[]{:S(2)}) collective-permute-start(f32[2,64,256]{2,1,0:T(8,128)S(1)} %get-tuple-element.116), channel_id=1, source_target_pairs={{32,0},{64,32},{96,64},{128,96},{160,128},{192,160},{224,192},{33,... | collective-permute-start | bytes 393224 | tf_op jit(solution)/shard_map/ppermute | solution.py:18
  50.3 8.8 %collective-permute-start.2 = (f32[2,384,64]{2,1,0:T(8,128)S(1)}, f32[2,384,64]{2,1,0:T(8,128)S(1)}, u32[]{:S(2)}, u32[]{:S(2)}) collective-permute-start(f32[2,384,64]{2,1,0:T(8,128)S(1)} %get-tuple-element.76), channel_id=1, source_target_pairs={{0,1},{1,2},{2,3},{3,4},{4,5},{5,6},{6,7},{7,8},{8,9},{9,10},{10,1... | collective-permute-start | bytes 589832 | tf_op jit(solution)/shard_map/ppermute | solution.py:15
  54.4 9.1 %collective-permute-start.3 = (f32[2,384,64]{2,1,0:T(8,128)S(1)}, f32[2,384,64]{2,1,0:T(8,128)S(1)}, u32[]{:S(2)}, u32[]{:S(2)}) collective-permute-start(f32[2,384,64]{2,1,0:T(8,128)S(1)} %get-tuple-element.77), channel_id=1, source_target_pairs={{1,0},{2,1},{3,2},{4,3},{5,4},{6,5},{7,6},{8,7},{9,8},{10,9},{11,1... | collective-permute-start | bytes 589832 | tf_op jit(solution)/shard_map/ppermute | solution.py:18
  57.1 32.5 %copy-start.10 = (f32[4,128,128]{2,1,0:T(8,128)}, f32[4,128,128]{2,1,0:T(8,128)S(1)}, u32[]{:S(2)}) copy-start(f32[4,128,128]{2,1,0:T(8,128)S(1)} %get-tuple-element.114) | copy-start | bytes 786436
  151.4 6.2 collective-permute-start.4
  155.0 7.3 collective-permute-start.5
  163.4 9.2 %collective-permute-start.6 = (f32[2,512,64]{2,1,0:T(8,128)}, f32[2,512,64]{2,1,0:T(8,128)S(1)}, u32[]{:S(2)}, u32[]{:S(2)}) collective-permute-start(f32[2,512,64]{2,1,0:T(8,128)} %get-tuple-element.60), channel_id=1, source_target_pairs={{0,1},{1,2},{2,3},{3,4},{4,5},{5,6},{6,7},{7,8},{8,9},{9,10},{10,1... | collective-permute-start | bytes 786440 | tf_op jit(solution)/shard_map/ppermute | solution.py:15
  166.2 10.8 %collective-permute-start.7 = (f32[2,512,64]{2,1,0:T(8,128)}, f32[2,512,64]{2,1,0:T(8,128)}, u32[]{:S(2)}, u32[]{:S(2)}) collective-permute-start(f32[2,512,64]{2,1,0:T(8,128)} %get-tuple-element.61), channel_id=1, source_target_pairs={{1,0},{2,1},{3,2},{4,3},{5,4},{6,5},{7,6},{8,7},{9,8},{10,9},{11,1... | collective-permute-start | bytes 786440 | tf_op jit(solution)/shard_map/ppermute | solution.py:18
  182.4 28.8 %copy-start.15 = (f32[4,128,128]{2,1,0:T(8,128)S(1)}, f32[4,128,128]{2,1,0:T(8,128)}, u32[]{:S(2)}) copy-start(f32[4,128,128]{2,1,0:T(8,128)} %get-tuple-element.22) | copy-start | bytes 786436
  182.4 28.8 %copy-start.16 = (f32[4,128,128]{2,1,0:T(8,128)S(1)}, f32[4,128,128]{2,1,0:T(8,128)}, u32[]{:S(2)}) copy-start(f32[4,128,128]{2,1,0:T(8,128)} %get-tuple-element.25) | copy-start | bytes 786436
  182.4 11.0 %collective-permute-start.8 = (f32[2,64,256]{2,1,0:T(8,128)S(1)}, f32[2,64,256]{2,1,0:T(8,128)S(1)}, u32[]{:S(2)}, u32[]{:S(2)}) collective-permute-start(f32[2,64,256]{2,1,0:T(8,128)S(1)} %get-tuple-element.96), channel_id=1, source_target_pairs={{0,32},{32,64},{64,96},{96,128},{128,160},{160,192},{192,224},{1,3... | collective-permute-start | bytes 393224 | tf_op jit(solution)/shard_map/ppermute | solution.py:15
  191.5 13.0 %collective-permute-start.9 = (f32[2,64,256]{2,1,0:T(8,128)S(1)}, f32[2,64,256]{2,1,0:T(8,128)S(1)}, u32[]{:S(2)}, u32[]{:S(2)}) collective-permute-start(f32[2,64,256]{2,1,0:T(8,128)S(1)} %get-tuple-element.97), channel_id=1, source_target_pairs={{32,0},{64,32},{96,64},{128,96},{160,128},{192,160},{224,192},{33,... | collective-permute-start | bytes 393224 | tf_op jit(solution)/shard_map/ppermute | solution.py:18
  205.6 8.6 %collective-permute-start.10 = (f32[2,384,64]{2,1,0:T(8,128)}, f32[2,384,64]{2,1,0:T(8,128)}, u32[]{:S(2)}, u32[]{:S(2)}) collective-permute-start(f32[2,384,64]{2,1,0:T(8,128)} %get-tuple-element.74), channel_id=1, source_target_pairs={{0,1},{1,2},{2,3},{3,4},{4,5},{5,6},{6,7},{7,8},{8,9},{9,10},{10,1... | collective-permute-start | bytes 589832 | tf_op jit(solution)/shard_map/ppermute | solution.py:15
  209.2 9.4 %collective-permute-start.11 = (f32[2,384,64]{2,1,0:T(8,128)}, f32[2,384,64]{2,1,0:T(8,128)}, u32[]{:S(2)}, u32[]{:S(2)}) collective-permute-start(f32[2,384,64]{2,1,0:T(8,128)} %get-tuple-element.75), channel_id=1, source_target_pairs={{1,0},{2,1},{3,2},{4,3},{5,4},{6,5},{7,6},{8,7},{9,8},{10,9},{11,1... | collective-permute-start | bytes 589832 | tf_op jit(solution)/shard_map/ppermute | solution.py:18
  212.0 38.2 %copy-start.6 = (f32[8,2,128,128]{3,2,0,1:T(8,128)S(1)}, f32[8,2,128,128]{3,2,0,1:T(8,128)}, u32[]{:S(2)}) copy-start(f32[8,2,128,128]{3,2,0,1:T(8,128)} %copy-done.5) | copy-start | bytes 3145732
  252.3 593.1 %all-reduce.5.cloned.1.call-start = ((), (), s32[]{:S(2)}) async-start(), calls=%async_computation | async-start | bytes 1179648 | tf_op jit(solution)/shard_map/psum | solution.py:130
  253.9 268.5 %copy-start.1 = (f32[8,128,128]{2,1,0:T(8,128)}, f32[8,128,128]{2,1,0:T(8,128)S(1)}, u32[]{:S(2)}) copy-start(f32[8,128,128]{2,1,0:T(8,128)S(1)} %slice_bitcast_fusion) | copy-start | bytes 1572868
  255.2 267.3 %copy-start.2 = (f32[8,128,128]{2,1,0:T(8,128)}, f32[8,128,128]{2,1,0:T(8,128)S(1)}, u32[]{:S(2)}) copy-start(f32[8,128,128]{2,1,0:T(8,128)S(1)} %slice_bitcast_fusion.1) | copy-start | bytes 1572868
  583.4 5.5 collective-permute-start.12
  585.8 8.2 collective-permute-start.13
  595.1 252.2 %collective-permute-start.14 = (f32[2,512,64]{2,1,0:T(8,128)}, f32[2,512,64]{2,1,0:T(8,128)S(1)}, u32[]{:S(2)}, u32[]{:S(2)}) collective-permute-start(f32[2,512,64]{2,1,0:T(8,128)} %get-tuple-element.56), channel_id=1, source_target_pairs={{0,1},{1,2},{2,3},{3,4},{4,5},{5,6},{6,7},{7,8},{8,9},{9,10},{10,1... | collective-permute-start | bytes 786440 | tf_op jit(solution)/shard_map/ppermute | solution.py:15
  600.3 247.1 %collective-permute-start.15 = (f32[2,512,64]{2,1,0:T(8,128)}, f32[2,512,64]{2,1,0:T(8,128)S(1)}, u32[]{:S(2)}, u32[]{:S(2)}) collective-permute-start(f32[2,512,64]{2,1,0:T(8,128)} %get-tuple-element.57), channel_id=1, source_target_pairs={{1,0},{2,1},{3,2},{4,3},{5,4},{6,5},{7,6},{8,7},{9,8},{10,9},{11,1... | collective-permute-start | bytes 786440 | tf_op jit(solution)/shard_map/ppermute | solution.py:18
  (14 other events, 90.2 us)
Sparse Core Ops, SparseCore 0:
  252.5 268.1 all-reduce.6
  588.1 257.2 all-reduce.4
where the time goes:
time: 862 us; the launch traced here: 857 us
  waiting for transfers between devices  553 us (64%)
  local copies, waits for them, and re-layouts  119 us (14%)
  matrix products  50.5 us (6%)
  starting transfers between devices  48 us (6%)
  between operations  46.7 us (5%)
  other arithmetic  39.4 us (5%)
    psum x2, waiting for transfers between devices, on_device(): gradient_sum, weight_sum = lax.psum((gradient, weight), ('row', 'col'))  509 us
    gather x48, local copies, waits for them, and re-layouts  53.1 us
    dot_general x8, matrix products, apply_table(): jnp.dot(flattened, table, precision=lax.Precision.HIGHEST, preferred_elem...  50.5 us
    dynamic_update_slice x16, local copies, waits for them, and re-layouts, on_device(): updates = lax.dynamic_update_slice(updates, current + contribution, corner)  38.4 us
    ppermute x8, starting transfers between devices, padded_2(): lax.ppermute(lax.slice_in_dim(block, block.shape[dim] - width, None, axis...  34.6 us
    ppermute x8, waiting for transfers between devices, padded_2(): lax.ppermute(lax.slice_in_dim(block, 0, width, axis=dim), axis, backward)  34.1 us
  transfers between devices with their start and end apart: 18, of which 14 were waited for; matrix products, arithmetic and copies ran while one was open for 2% of the time, Pallas kernels for 0%

commit v1 on v0

--- a/solution.py
+++ b/solution.py
@@ -5,6 +5,11 @@
 from jax.sharding import PartitionSpec as P
 
 PASSES = 2
+
+
+def by_each_axis(array, one, other):
+    half = lax.psum(array, one)
+    return lax.psum(half, other)
 
 
 def padded_2(block, sides, width):
@@ -127,7 +132,7 @@
         tile_sum = fold_rim(fold_rim(summed, 1, tile_rows, rim_width), 2, tile_cols, rim_width)
         probe_peak = jnp.max(jnp.sum(probe_now[0] ** 2 + probe_now[1] ** 2, axis=0))
         object_now = object_now + tile_sum / probe_peak
-        gradient_sum, weight_sum = lax.psum((gradient, weight), ("row", "col"))
+        gradient_sum, weight_sum = by_each_axis((gradient, weight), "row", "col")
         probe_now = probe_now + gradient_sum / weight_sum[None, None]
     return (object_now, probe_now)
 

time: 862 us -> 1110 us (1.29)
  waiting for transfers between devices: 553 us -> 794 us
    psum x2 -> x4, waiting for transfers between devices: 509 us -> 744 us  [the longest x2 536 us: by_each_axis(): return lax.psum(half, other)]
  transfers between devices with their start and end apart: 18 -> 20, of which waited for: 14 -> 18; matrix products, arithmetic and copies ran while one was open for 2% -> 2% of each run, Pallas kernels for 0% -> 0%
where the time goes in v1:
time: 1110 us; the launch traced here: 1100 us
  waiting for transfers between devices  794 us (72%)
  local copies, waits for them, and re-layouts  121 us (11%)
  matrix products  50.5 us (5%)
  starting transfers between devices  48.5 us (4%)
  between operations  46.1 us (4%)
  other arithmetic  42 us (4%)
    psum x2, waiting for transfers between devices, by_each_axis(): return lax.psum(half, other)  536 us
    psum x2, waiting for transfers between devices, by_each_axis(): half = lax.psum(array, one)  209 us
    gather x48, local copies, waits for them, and re-layouts  54.4 us
    dot_general x8, matrix products, apply_table(): jnp.dot(flattened, table, precision=lax.Precision.HIGHEST, preferred_elem...  50.5 us
    dynamic_update_slice x16, local copies, waits for them, and re-layouts, on_device(): updates = lax.dynamic_update_slice(updates, current + contribution, corner)  38.4 us
    ppermute x8, waiting for transfers between devices, padded_2(): lax.ppermute(lax.slice_in_dim(block, 0, width, axis=dim), axis, backward)  37.7 us
    ppermute x8, starting transfers between devices, padded_2(): lax.ppermute(lax.slice_in_dim(block, block.shape[dim] - width, None, axis...  32.5 us
  transfers between devices with their start and end apart: 20, of which 18 were waited for; matrix products, arithmetic and copies ran while one was open for 2% of the time, Pallas kernels for 0%

profile of v1, /device:TPU:1, one launch (start us, length us, event | category | flops | bytes accessed | tf_op | source)
XLA Modules:
  0.0 1102.1 jit_solution(13699451702411389352)
XLA Ops:
  50.0 4.0 collective-permute-start.2
  58.8 4.4 collective-permute-done.3
  64.7 25.0 %while.2 = (s32[]{:T(128)}, f32[2,384,384]{2,1,0:T(8,128)}, s32[8,3]{0,1:T(4,128)S(1)}, f32[8,2,128,128]{3,2,0,1:T(8,128)S(1)}, s32[]{:T(128)}) while((s32[]{:T(128)}, f32[2,384,384]{2,1,0:T(8,128)}, s32[8,3]{0,1:T(4,128)S(1)}, f32[8,2,128,128]{3,2,0,1:T(8,128)S(1)}, s32[]{:T(128)}) %tuple.107), condition=%wide.while_cond, body=%wide.while_body.sunk | while | flops 2 | bytes 262261 | solution.py:91
  94.7 7.1 fusion.47
  104.8 7.1 fusion.48
  111.9 7.3 fusion.49
  126.4 4.9 add_reduce_fusion.2
  157.8 4.7 collective-permute-done.5
  172.8 4.4 collective-permute-done.7
  182.7 9.1 collective-permute-start.8
  193.7 11.1 %collective-permute-done.9 = f32[2,64,256]{2,1,0:T(8,128)S(1)} collective-permute-done((f32[2,64,256]{2,1,0:T(8,128)S(1)}, f32[2,64,256]{2,1,0:T(8,128)S(1)}, u32[]{:S(2)}, u32[]{:S(2)}) %collective-permute-start.9) | collective-permute-done | bytes 131104 | tf_op jit(solution)/shard_map/ppermute | solution.py:23
  214.5 4.4 collective-permute-done.11
  221.5 29.8 %while.3 = (s32[]{:T(128)}, f32[2,384,384]{2,1,0:T(8,128)}, s32[8,3]{0,1:T(4,128)S(1)}, f32[8,2,128,128]{3,2,1,0:T(8,128)}, s32[]{:T(128)}) while((s32[]{:T(128)}, f32[2,384,384]{2,1,0:T(8,128)}, s32[8,3]{0,1:T(4,128)S(1)}, f32[8,2,128,128]{3,2,1,0:T(8,128)}, s32[]{:T(128)}) %tuple.125), condition=%wide.while_cond.1, body=%wide.while_body.1.sunk | while | flops 2 | bytes 263785 | solution.py:91
  253.5 119.5 %all-reduce.15.cloned.1.call-done = (f32[2,4,128,128]{3,2,1,0:T(8,128)}, f32[128,128]{1,0:T(8,128)}) async-done(((f32[2,4,128,128]{3,2,1,0:T(8,128)}, f32[128,128]{1,0:T(8,128)}), (f32[2,4,128,128]{3,2,1,0:T(8,128)}, f32[128,128]{1,0:T(8,128)})) %all-reduce.15.cloned.1.call-update) | async-done | bytes 589840 | tf_op jit(solution)/shard_map/psum | solution.py:11
  375.8 268.3 %all-reduce.11.cloned.1.call-done = (f32[2,4,128,128]{3,2,1,0:T(8,128)}, f32[128,128]{1,0:T(8,128)}) async-done(((f32[2,4,128,128]{3,2,1,0:T(8,128)}, f32[128,128]{1,0:T(8,128)}), (f32[2,4,128,128]{3,2,1,0:T(8,128)}, f32[128,128]{1,0:T(8,128)})) %all-reduce.11.cloned.1.call-update) | async-done | bytes 589840 | tf_op jit(solution)/shard_map/psum | solution.py:12
  649.8 7.1 fusion.50
  659.4 7.1 fusion.51
  666.5 7.4 fusion.52
  681.0 4.8 add_reduce_fusion
  712.2 4.4 collective-permute-done.13
  720.8 4.5 collective-permute-start.15
  727.2 4.3 collective-permute-done.15
  733.4 89.1 %all-reduce.13.cloned.1.call-done = (f32[2,4,128,128]{3,2,1,0:T(8,128)}, f32[128,128]{1,0:T(8,128)}) async-done(((f32[2,4,128,128]{3,2,1,0:T(8,128)}, f32[128,128]{1,0:T(8,128)}), (f32[2,4,128,128]{3,2,1,0:T(8,128)}, f32[128,128]{1,0:T(8,128)})) %all-reduce.13.cloned.1.call-update) | async-done | bytes 589840 | tf_op jit(solution)/shard_map/psum | solution.py:11
  825.9 267.6 %all-reduce.9.cloned.1.call-done = (f32[2,4,128,128]{3,2,1,0:T(8,128)}, f32[128,128]{1,0:T(8,128)}) async-done(((f32[2,4,128,128]{3,2,1,0:T(8,128)}, f32[128,128]{1,0:T(8,128)}), (f32[2,4,128,128]{3,2,1,0:T(8,128)}, f32[128,128]{1,0:T(8,128)})) %all-reduce.9.cloned.1.call-update) | async-done | bytes 589840 | tf_op jit(solution)/shard_map/psum | solution.py:12
  (227 shorter events, 203.1 us)
Async XLA Ops:
  7.2 365.8 %all-reduce.15.cloned.1.call-start = ((), (), s32[]{:S(2)}) async-start(), calls=%async_computation.3 | async-start | bytes 1179648 | tf_op jit(solution)/shard_map/psum | solution.py:11
  8.2 40.5 %collective-permute-start = (f32[2,64,256]{2,1,0:T(8,128)S(1)}, f32[2,64,256]{2,1,0:T(8,128)S(1)}, u32[]{:S(2)}, u32[]{:S(2)}) collective-permute-start(f32[2,64,256]{2,1,0:T(8,128)S(1)} %get-tuple-element.121), channel_id=1, source_target_pairs={{0,32},{32,64},{64,96},{96,128},{128,160},{160,192},{192,224},{1,3... | collective-permute-start | bytes 393224 | tf_op jit(solution)/shard_map/ppermute | solution.py:20
  12.2 37.7 %collective-permute-start.1 = (f32[2,64,256]{2,1,0:T(8,128)S(1)}, f32[2,64,256]{2,1,0:T(8,128)S(1)}, u32[]{:S(2)}, u32[]{:S(2)}) collective-permute-start(f32[2,64,256]{2,1,0:T(8,128)S(1)} %get-tuple-element.120), channel_id=1, source_target_pairs={{32,0},{64,32},{96,64},{128,96},{160,128},{192,160},{224,192},{33,... | collective-permute-start | bytes 393224 | tf_op jit(solution)/shard_map/ppermute | solution.py:23
  50.0 8.8 collective-permute-start.2
  54.1 9.1 collective-permute-start.3
  56.8 33.0 %copy-start.10 = (f32[4,128,128]{2,1,0:T(8,128)}, f32[4,128,128]{2,1,0:T(8,128)S(1)}, u32[]{:S(2)}) copy-start(f32[4,128,128]{2,1,0:T(8,128)S(1)} %get-tuple-element.118) | copy-start | bytes 786436
  151.6 6.2 collective-permute-start.4
  155.2 7.3 collective-permute-start.5
  163.6 9.2 collective-permute-start.6
  166.4 10.8 collective-permute-start.7
  182.7 11.0 %collective-permute-start.8 = (f32[2,64,256]{2,1,0:T(8,128)S(1)}, f32[2,64,256]{2,1,0:T(8,128)S(1)}, u32[]{:S(2)}, u32[]{:S(2)}) collective-permute-start(f32[2,64,256]{2,1,0:T(8,128)S(1)} %get-tuple-element.100), channel_id=1, source_target_pairs={{0,32},{32,64},{64,96},{96,128},{128,160},{160,192},{192,224},{1,3... | collective-permute-start | bytes 393224 | tf_op jit(solution)/shard_map/ppermute | solution.py:20
  191.8 13.0 %collective-permute-start.9 = (f32[2,64,256]{2,1,0:T(8,128)S(1)}, f32[2,64,256]{2,1,0:T(8,128)S(1)}, u32[]{:S(2)}, u32[]{:S(2)}) collective-permute-start(f32[2,64,256]{2,1,0:T(8,128)S(1)} %get-tuple-element.101), channel_id=1, source_target_pairs={{32,0},{64,32},{96,64},{128,96},{160,128},{192,160},{224,192},{33,... | collective-permute-start | bytes 393224 | tf_op jit(solution)/shard_map/ppermute | solution.py:23
  205.9 8.6 collective-permute-start.10
  209.5 9.4 collective-permute-start.11
  212.3 39.0 %copy-start.6 = (f32[8,2,128,128]{3,2,0,1:T(8,128)S(1)}, f32[8,2,128,128]{3,2,0,1:T(8,128)}, u32[]{:S(2)}) copy-start(f32[8,2,128,128]{3,2,0,1:T(8,128)} %copy-done.5) | copy-start | bytes 3145732
  253.4 390.7 %all-reduce.11.cloned.1.call-start = ((), (), s32[]{:S(2)}) async-start(), calls=%async_computation.1 | async-start | bytes 1179648 | tf_op jit(solution)/shard_map/psum | solution.py:12
  373.0 449.5 %all-reduce.13.cloned.1.call-start = ((), (), s32[]{:S(2)}) async-start(), calls=%async_computation.2 | async-start | bytes 1179648 | tf_op jit(solution)/shard_map/psum | solution.py:11
  374.5 271.3 %copy-start.1 = (f32[8,128,128]{2,1,0:T(8,128)}, f32[8,128,128]{2,1,0:T(8,128)S(1)}, u32[]{:S(2)}) copy-start(f32[8,128,128]{2,1,0:T(8,128)S(1)} %slice_bitcast_fusion) | copy-start | bytes 1572868
  375.8 270.1 %copy-start.2 = (f32[8,128,128]{2,1,0:T(8,128)}, f32[8,128,128]{2,1,0:T(8,128)S(1)}, u32[]{:S(2)}) copy-start(f32[8,128,128]{2,1,0:T(8,128)S(1)} %slice_bitcast_fusion.1) | copy-start | bytes 1572868
  706.9 5.3 collective-permute-start.12
  709.3 7.3 collective-permute-start.13
  711.5 382.0 %all-reduce.9.cloned.1.call-start = ((), (), s32[]{:S(2)}) async-start(), calls=%async_computation | async-start | bytes 1179648 | tf_op jit(solution)/shard_map/psum | solution.py:12
  717.7 9.5 collective-permute-start.14
  720.8 10.7 collective-permute-start.15
  (16 other events, 152.5 us)
Sparse Core Ops, SparseCore 0:
  253.5 119.3 all-reduce.14
  375.7 268.3 all-reduce.10
  711.6 110.8 all-reduce.12
  825.0 268.3 all-reduce.8
